TPU v7x, 32 devices: a whole 2x2x4 slice. The times are simulated.
32 devices in a mesh: groups: 2 (over x), spatial: 16 (over z, y, core).
Axes of the slice: x: 2, y: 2, z: 4, core: 2. Of those that a mesh axis runs over, the one named last changes fastest.
Arguments:
- fields: bfloat16 [1024, 128, 768], P(('groups', 'spatial')), parts along dimension 0, may hold values from -6 to 6
- norm1_gain: float32 [768], replicated, may hold values from 0.5 to 1.5
- norm1_bias: float32 [768], replicated, may hold values from -3 to 3
- spectral_w1: float32 [2, 8, 96, 96], replicated, may hold values from -0.4375 to 0.4375
- spectral_b1: float32 [2, 8, 96], replicated, may hold values from -3 to 3
- spectral_w2: float32 [2, 8, 96, 96], replicated, may hold values from -0.4375 to 0.4375
- spectral_b2: float32 [2, 8, 96], replicated, may hold values from -3 to 3
- norm2_gain: float32 [768], replicated, may hold values from 0.5 to 1.5
- norm2_bias: float32 [768], replicated, may hold values from -3 to 3
- fc1_weight: bfloat16 [768, 3072], replicated, may hold values from -0.21875 to 0.21875
- fc1_bias: float32 [3072], replicated, may hold values from -3 to 3
- fc2_weight: bfloat16 [3072, 768], replicated, may hold values from -0.109375 to 0.109375
- fc2_bias: float32 [768], replicated, may hold values from -3 to 3
Outputs:
- next_state: bfloat16 [1024, 128, 768], P(('groups', 'spatial')), parts along dimension 0
- anomaly: bfloat16 [1024, 128, 768], P(('groups', 'spatial')), parts along dimension 0
There are 2 independent parts, one for each index of `groups`. A program takes and returns all parts, laid end to end along the dimension named above; an argument that names none is the same for every part. Nothing has to cross between parts.
All inputs are finite; a program needn't handle non-finite values.
Results may differ from a plain program's by a relative error of at most 0.0056.
Values may be sent and summed in bfloat16 or wider, within the bound.
A program may use at most 192 MiB of HBM per device.

v0:
```python
import math
import jax
import jax.numpy as jnp
from jax import lax
from jax.sharding import Mesh, PartitionSpec as P

MEMBERS = 8
EPSILON = 1e-06
SHRINK = 0.01
FULL_PRECISION = lax.Precision.HIGHEST


def from_behind(block, axis, distance):
    devices = range(lax.axis_size(axis))
    route = [((i - distance) % len(devices), i) for i in devices]
    return lax.ppermute(block, axis, route)


def layer_norm(values, gain, offset_term):
    center = values - jnp.mean(values, axis=-1, keepdims=True)
    spread = jnp.mean(center * center, axis=-1, keepdims=True)
    return center * lax.rsqrt(spread + EPSILON) * gain + offset_term


def soft_shrink(values):
    return jnp.where(
        values > SHRINK, values - SHRINK, jnp.where(values < -SHRINK, values + SHRINK, 0.0)
    )


def contract(form, left, right):
    return jnp.einsum(form, left, right, precision=FULL_PRECISION)


def block_product(values, weight):
    return jnp.einsum("...bi,bio->...bo", values, weight, precision=FULL_PRECISION)


def angle_table(first_len, second_len, modulus):
    first_index = lax.broadcasted_iota(jnp.int32, (first_len, second_len), 0)
    second_index = lax.broadcasted_iota(jnp.int32, (first_len, second_len), 1)
    phase = first_index * second_index % modulus
    return phase.astype(jnp.float32) * (2.0 * math.pi / modulus)


def spectral_layer(real_part, imag_part, w_first, b_first, w_second, b_second):
    shape = real_part.shape
    block_count = w_first.shape[1]
    split_shape = shape[:-1] + (block_count, shape[-1] // block_count)
    real_part = real_part.reshape(split_shape)
    imag_part = imag_part.reshape(split_shape)
    hidden_real = jax.nn.relu(
        block_product(real_part, w_first[0]) - block_product(imag_part, w_first[1]) + b_first[0]
    )
    hidden_imag = jax.nn.relu(
        block_product(imag_part, w_first[0]) + block_product(real_part, w_first[1]) + b_first[1]
    )
    mixed_real = (
        block_product(hidden_real, w_second[0])
        - block_product(hidden_imag, w_second[1])
        + b_second[0]
    )
    mixed_imag = (
        block_product(hidden_imag, w_second[0])
        + block_product(hidden_real, w_second[1])
        + b_second[1]
    )
    return (soft_shrink(mixed_real).reshape(shape), soft_shrink(mixed_imag).reshape(shape))


def longitude_forward(normed, lon_len):
    angles = angle_table(lon_len, lon_len // 2, lon_len)
    factor = 1.0 / math.sqrt(lon_len)
    real_part = contract("rld,lk->rkd", normed, jnp.cos(angles) * factor)
    imag_part = -contract("rld,lk->rkd", normed, jnp.sin(angles) * factor)
    return (real_part, imag_part)


def longitude_inverse(real_part, imag_part, lon_len):
    half_len = lon_len // 2
    angles = angle_table(lon_len, half_len, lon_len)
    column_index = lax.broadcasted_iota(jnp.int32, (1, half_len), 1)
    weights = jnp.where(column_index == 0, 1.0, 2.0) / math.sqrt(lon_len)
    cosine_table = jnp.cos(angles) * weights
    sine_table = jnp.sin(angles) * weights
    return contract("rkd,lk->rld", real_part, cosine_table) - contract(
        "rkd,lk->rld", imag_part, sine_table
    )


def latitude_work(real_part, imag_part, w_first, b_first, w_second, b_second):
    member_rows, mode_count, channels = real_part.shape
    lat_len = member_rows // MEMBERS
    angles = angle_table(lat_len, lat_len, lat_len)
    factor = 1.0 / math.sqrt(lat_len)
    cosine_table = jnp.cos(angles) * factor
    sine_table = jnp.sin(angles) * factor
    grid_real = real_part.reshape(MEMBERS, lat_len, mode_count, channels)
    grid_imag = imag_part.reshape(MEMBERS, lat_len, mode_count, channels)
    spec_real = contract("qp,mpkd->mqkd", cosine_table, grid_real) + contract(
        "qp,mpkd->mqkd", sine_table, grid_imag
    )
    spec_imag = contract("qp,mpkd->mqkd", cosine_table, grid_imag) - contract(
        "qp,mpkd->mqkd", sine_table, grid_real
    )
    mixed_real, mixed_imag = spectral_layer(
        spec_real, spec_imag, w_first, b_first, w_second, b_second
    )
    back_real = contract("qp,mpkd->mqkd", cosine_table, mixed_real) - contract(
        "qp,mpkd->mqkd", sine_table, mixed_imag
    )
    back_imag = contract("qp,mpkd->mqkd", cosine_table, mixed_imag) + contract(
        "qp,mpkd->mqkd", sine_table, mixed_real
    )
    return (
        back_real.reshape(member_rows, mode_count, channels),
        back_imag.reshape(member_rows, mode_count, channels),
    )


def on_device(
    fields,
    norm1_gain,
    norm1_bias,
    spectral_w1,
    spectral_b1,
    spectral_w2,
    spectral_b2,
    norm2_gain,
    norm2_bias,
    fc1_weight,
    fc1_bias,
    fc2_weight,
    fc2_bias,
):
    row_count, lon_len, channels = fields.shape
    state = fields.astype(jnp.float32)
    normed = layer_norm(state, norm1_gain, norm1_bias)
    real_part, imag_part = longitude_forward(normed, lon_len)
    real_part, imag_part = (
        lax.all_to_all(real_part, "spatial", split_axis=1, concat_axis=0, tiled=True),
        lax.all_to_all(imag_part, "spatial", split_axis=1, concat_axis=0, tiled=True),
    )
    real_part, imag_part = latitude_work(
        real_part, imag_part, spectral_w1, spectral_b1, spectral_w2, spectral_b2
    )
    real_part, imag_part = (
        lax.all_to_all(real_part, "spatial", split_axis=0, concat_axis=1, tiled=True),
        lax.all_to_all(imag_part, "spatial", split_axis=0, concat_axis=1, tiled=True),
    )
    filtered = longitude_inverse(real_part, imag_part, lon_len)
    residual = (filtered + normed + state).reshape(row_count * lon_len, channels)
    normed2 = layer_norm(residual, norm2_gain, norm2_bias).astype(jnp.bfloat16)
    hidden = jax.nn.gelu(
        jnp.dot(normed2, fc1_weight, preferred_element_type=jnp.float32) + fc1_bias,
        approximate=False,
    ).astype(jnp.bfloat16)
    updated = residual + jnp.dot(hidden, fc2_weight, preferred_element_type=jnp.float32) + fc2_bias
    next_state = updated.astype(jnp.bfloat16).reshape(row_count, lon_len, channels)
    return next_state


def ensemble_step(next_state):
    state_values = next_state.astype(jnp.float32)
    summed = lax.psum(state_values, "member")
    anomaly = (state_values - summed / MEMBERS).astype(jnp.bfloat16)
    return (next_state, anomaly)


def solution(mesh):
    placed = (
        P(("groups", "spatial"), None, None),
        P(),
        P(),
        P(),
        P(),
        P(),
        P(),
        P(),
        P(),
        P(),
        P(),
        P(),
        P(),
    )
    update = jax.shard_map(
        on_device,
        mesh=mesh,
        in_specs=placed,
        out_specs=P(("groups", "spatial"), None, None),
        check_vma=False,
    )
    member_span = mesh.shape["spatial"] // MEMBERS
    ensemble_mesh = Mesh(
        mesh.devices.reshape(mesh.shape["groups"], MEMBERS, member_span),
        ("groups", "member", "half"),
    )
    member_rows = P(("groups", "member", "half"), None, None)
    spread = jax.shard_map(
        ensemble_step,
        mesh=ensemble_mesh,
        in_specs=(member_rows,),
        out_specs=(member_rows, member_rows),
        check_vma=False,
    )

    def step(*args):
        return spread(update(*args))

    return step
```

profile of v0, /device:TPU:0, one launch (start us, length us, event | category | flops | bytes accessed | tf_op | source)
XLA Modules:
  0.0 1506.0 jit_solution(8603126026089970054)
XLA Ops:
  7.6 9.6 negate_bitcast_fusion
  31.3 12.0 fusion.94
  49.6 95.7 %all-to-all-done.1 = f32[32,64,768]{2,0,1:T(8,128)} async-done(((f32[32,64,768]{2,0,1:T(8,128)}), f32[32,64,768]{2,0,1:T(8,128)}, u32[]{:S(2)}, u32[]{:S(2)}) %all-to-all-start.1) | async-done | bytes 6291488 | tf_op jit(solution)/shard_map/all_to_all | solution.py:142
  145.3 28.5 %all-to-all-start = ((f32[32,64,768]{2,0,1:T(8,128)}), f32[32,64,768]{2,0,1:T(8,128)}, u32[]{:S(2)}, u32[]{:S(2)}) async-start(f32[32,64,768]{2,0,1:T(8,128)} %copy.57), calls=%async_computation | async-start | bytes 12582912 | tf_op jit(solution)/shard_map/all_to_all | solution.py:141
  193.1 94.8 %all-to-all-done = f32[32,64,768]{2,0,1:T(8,128)} async-done(((f32[32,64,768]{2,0,1:T(8,128)}), f32[32,64,768]{2,0,1:T(8,128)}, u32[]{:S(2)}, u32[]{:S(2)}) %all-to-all-start) | async-done | bytes 6291488 | tf_op jit(solution)/shard_map/all_to_all | solution.py:141
  302.2 9.9 reshape.102
  312.1 13.7 fusion.58
  325.9 9.9 fusion.60
  343.9 9.9 reshape.101
  353.8 13.1 add_maximum_fusion
  367.0 9.5 fusion.50
  376.5 9.9 fusion.52
  386.4 9.6 add_maximum_fusion.1
  396.0 14.9 select_bitcast_fusion
  410.9 10.9 copy.70
  421.9 9.6 reshape.104
  431.5 12.2 select_bitcast_fusion.1
  443.7 10.9 copy.69
  454.7 9.6 reshape.103
  464.2 8.3 fusion.128
  472.5 8.7 subtract_bitcast_fusion
  488.4 28.2 %all-to-all-start.2 = ((f32[512,4,768]{2,1,0:T(4,128)}), f32[512,4,768]{2,1,0:T(4,128)}, u32[]{:S(2)}, u32[]{:S(2)}) async-start(f32[512,4,768]{2,1,0:T(4,128)} %copy.72), calls=%async_computation.2 | async-start | bytes 12582912 | tf_op jit(solution)/shard_map/all_to_all | solution.py:148
  516.7 8.6 fusion.126
  539.2 91.6 %all-to-all-done.2 = f32[512,4,768]{2,1,0:T(4,128)} async-done(((f32[512,4,768]{2,1,0:T(4,128)}), f32[512,4,768]{2,1,0:T(4,128)}, u32[]{:S(2)}, u32[]{:S(2)}) %all-to-all-start.2) | async-done | bytes 6291488 | tf_op jit(solution)/shard_map/all_to_all | solution.py:148
  630.7 28.5 %all-to-all-start.3 = ((f32[512,4,768]{2,1,0:T(4,128)}), f32[512,4,768]{2,1,0:T(4,128)}, u32[]{:S(2)}, u32[]{:S(2)}) async-start(f32[512,4,768]{2,1,0:T(4,128)} %copy.76), calls=%async_computation.3 | async-start | bytes 12582912 | tf_op jit(solution)/shard_map/all_to_all | solution.py:149
  677.7 95.6 %all-to-all-done.3 = f32[512,4,768]{2,1,0:T(4,128)} async-done(((f32[512,4,768]{2,1,0:T(4,128)}), f32[512,4,768]{2,1,0:T(4,128)}, u32[]{:S(2)}, u32[]{:S(2)}) %all-to-all-start.3) | async-done | bytes 6291488 | tf_op jit(solution)/shard_map/all_to_all | solution.py:149
  792.0 15.1 %fusion.134 = f32[128,32,768]{2,0,1:T(8,128)} fusion(f32[32,64,768]{2,1,0:T(8,128)} %all_to_all.57, f32[64]{0:T(128)S(1)} %fusion.172), kind=kOutput, calls=%fused_computation.149 | convolution fusion | flops 2416041984 | bytes 18874624 | tf_op jit(solution)/shard_map/rkd,lk->rld/dot_general | solution.py:32
  807.1 19.1 %fusion.262 = (f32[32,128]{1,0:T(8,128)S(1)}, f32[32,128,768]{2,1,0:T(8,128)S(1)}) fusion(f32[768]{0:T(1024)S(1)} %copy-done.16, f32[768]{0:T(1024)S(1)} %copy-done.18, f32[32,128]{1,0:T(8,128)S(1)} %copy-done.12, f32[32,128]{1,0:T(8,128)S(1)} %copy-done.10, bf16[32,128,768]{2,1,0:T(8,128)(2,1)} %param.14, f32[128,32,768]{2,0,1:T(8,128)} %fusion.134, ...), kind=kOutput, calls=%fused_computation.276 | convolution fusion | flops 2444349440 | bytes 37804288 | tf_op jit(solution)/shard_map/rkd,lk->rld/dot_general | solution.py:32
  830.8 126.3 %fusion.2.clone.6 = bf16[4096,3072]{1,0:T(8,128)(2,1)} fusion(bf16[4096,768]{1,0:T(8,128)(2,1)S(1)} %fusion.47, bf16[768,3072]{1,0:T(8,128)(2,1)} %param.23, f32[3072]{0:T(1024)S(1)} %copy-done.21), kind=kOutput, calls=%fused_computation.3.clone.clone.clone.clone.clone.1 | convolution fusion | flops 20157825024 | bytes 36188160 | tf_op jit(solution)/shard_map/dot_general | solution.py:155
  957.2 27.6 %fusion.49 = bf16[4096,768]{1,0:T(8,128)(2,1)} fusion(f32[32,128,768]{2,1,0:T(8,128)} %copy-done, bf16[3072,768]{1,0:T(8,128)(2,1)} %param.25, f32[768]{0:T(1024)S(1)} %copy-done.22, bf16[4096,3072]{1,0:T(8,128)(2,1)} %fusion.2.clone.6), kind=kOutput, calls=%fused_computation.61 | convolution fusion | flops 19336790016 | bytes 48761856 | tf_op jit(solution)/shard_map/dot_general | solution.py:158
  984.7 509.6 %all-reduce.1 = f32[32,128,768]{2,1,0:T(8,128)} all-reduce(bf16[32,128,768]{2,1,0:T(8,128)(2,1)} %bitcast.202), channel_id=1, replica_groups=mesh['groups'=2,'member'=8,'half'=2] {'member'}, use_global_device_ids=true, to_apply=%region_4.6 | all-reduce | flops 3145728 | bytes 18874368 | tf_op jit(solution)/shard_map/psum | solution.py:165
  1494.3 11.2 subtract_convert_fusion
  (107 shorter events, 131.5 us)
Async XLA Ops:
  0.6 7.0 copy-start.15
  0.7 7.0 copy-start.17
  5.2 26.0 %copy-start.9 = (f32[32,128]{1,0:T(8,128)}, f32[32,128]{1,0:T(8,128)S(1)}, u32[]{:S(2)}) copy-start(f32[32,128]{1,0:T(8,128)S(1)} %broadcast_multiply_fusion.1) | copy-start | bytes 49156
  7.6 23.6 %copy-start.11 = (f32[32,128]{1,0:T(8,128)}, f32[32,128]{1,0:T(8,128)S(1)}, u32[]{:S(2)}) copy-start(f32[32,128]{1,0:T(8,128)S(1)} %add_rsqrt_fusion) | copy-start | bytes 49156
  23.8 121.5 %all-to-all-start.1 = ((f32[32,64,768]{2,0,1:T(8,128)}), f32[32,64,768]{2,0,1:T(8,128)}, u32[]{:S(2)}, u32[]{:S(2)}) async-start(f32[32,64,768]{2,0,1:T(8,128)} %copy.60), calls=%async_computation.1 | async-start | bytes 12582912 | tf_op jit(solution)/shard_map/all_to_all | solution.py:142
  49.6 124.2 %copy-start.13 = (f32[2,8,96]{2,1,0:T(8,128)S(1)}, f32[2,8,96]{2,1,0:T(8,128)}, u32[]{:S(2)}) copy-start(f32[2,8,96]{2,1,0:T(8,128)} %param.18) | copy-start | bytes 18436
  49.6 124.3 %copy-start.14 = (f32[2,8,96]{2,1,0:T(8,128)S(1)}, f32[2,8,96]{2,1,0:T(8,128)}, u32[]{:S(2)}) copy-start(f32[2,8,96]{2,1,0:T(8,128)} %param.20) | copy-start | bytes 18436
  145.3 142.6 %all-to-all-start = ((f32[32,64,768]{2,0,1:T(8,128)}), f32[32,64,768]{2,0,1:T(8,128)}, u32[]{:S(2)}, u32[]{:S(2)}) async-start(f32[32,64,768]{2,0,1:T(8,128)} %copy.57), calls=%async_computation | async-start | bytes 12582912 | tf_op jit(solution)/shard_map/all_to_all | solution.py:141
  193.1 101.2 %slice-start.10 = ((s8[6291456]{0:T(1024)(128)(4,1)}), s8[2097152]{0:T(1024)(128)(4,1)S(1)}, s32[]{:S(2)}) async-start(s8[6291456]{0:T(1024)(128)(4,1)} %bitcast.200), calls=%async_computation.14 | async-start | bytes 4194304
  302.2 9.9 copy-start.5
  312.1 13.8 copy-start.1
  312.1 23.6 %slice-start.4 = ((s8[6291456]{0:T(1024)(128)(4,1)}), s8[4194304]{0:T(1024)(128)(4,1)S(1)}, s32[]{:S(2)}) async-start(s8[6291456]{0:T(1024)(128)(4,1)} %bitcast.189), calls=%async_computation.8 | async-start | bytes 8388608
  312.1 23.6 %slice-start.8 = ((s8[6291456]{0:T(1024)(128)(4,1)}), s8[4194304]{0:T(1024)(128)(4,1)S(1)}, s32[]{:S(2)}) async-start(s8[6291456]{0:T(1024)(128)(4,1)} %bitcast.198), calls=%async_computation.12 | async-start | bytes 8388608
  325.9 9.9 slice-start.5
  325.9 9.9 slice-start.9
  353.8 13.2 copy-start.6
  367.0 9.5 copy-start.7
  367.0 19.4 %slice-start = ((s8[8388608]{0:T(1024)(128)(4,1)}), s8[4194304]{0:T(1024)(128)(4,1)S(1)}, s32[]{:S(2)}) async-start(s8[8388608]{0:T(1024)(128)(4,1)} %bitcast.182), calls=%async_computation.4 | async-start | bytes 8388608
  367.0 19.4 %slice-start.6 = ((s8[8388608]{0:T(1024)(128)(4,1)}), s8[4194304]{0:T(1024)(128)(4,1)S(1)}, s32[]{:S(2)}) async-start(s8[8388608]{0:T(1024)(128)(4,1)} %bitcast.192), calls=%async_computation.10 | async-start | bytes 8388608
  376.5 9.9 slice-start.1
  376.5 9.9 slice-start.7
  396.0 14.9 copy-start.2
  421.8 9.6 copy-start.8
  488.4 36.9 %slice-start.2 = ((s8[6291456]{0:T(1024)(128)(4,1)}), s8[2097152]{0:T(1024)(128)(4,1)S(1)}, s32[]{:S(2)}) async-start(s8[6291456]{0:T(1024)(128)(4,1)} %bitcast.184), calls=%async_computation.6 | async-start | bytes 4194304
  488.4 142.3 %all-to-all-start.2 = ((f32[512,4,768]{2,1,0:T(4,128)}), f32[512,4,768]{2,1,0:T(4,128)}, u32[]{:S(2)}, u32[]{:S(2)}) async-start(f32[512,4,768]{2,1,0:T(4,128)} %copy.72), calls=%async_computation.2 | async-start | bytes 12582912 | tf_op jit(solution)/shard_map/all_to_all | solution.py:148
  516.7 8.7 slice-start.3
  630.7 142.6 %all-to-all-start.3 = ((f32[512,4,768]{2,1,0:T(4,128)}), f32[512,4,768]{2,1,0:T(4,128)}, u32[]{:S(2)}, u32[]{:S(2)}) async-start(f32[512,4,768]{2,1,0:T(4,128)} %copy.76), calls=%async_computation.3 | async-start | bytes 12582912 | tf_op jit(solution)/shard_map/all_to_all | solution.py:149
  791.9 15.1 %copy-start.10 = (f32[32,128]{1,0:T(8,128)S(1)}, f32[32,128]{1,0:T(8,128)}, u32[]{:S(2)}) copy-start(f32[32,128]{1,0:T(8,128)} %copy-done.9) | copy-start | bytes 49156
  792.0 15.1 %copy-start.12 = (f32[32,128]{1,0:T(8,128)S(1)}, f32[32,128]{1,0:T(8,128)}, u32[]{:S(2)}) copy-start(f32[32,128]{1,0:T(8,128)} %copy-done.11) | copy-start | bytes 49156
  792.0 15.1 %copy-start.16 = (f32[768]{0:T(1024)S(1)}, f32[768]{0:T(1024)}, u32[]{:S(2)}) copy-start(f32[768]{0:T(1024)} %param.16) | copy-start | bytes 9220
  792.0 15.1 %copy-start.18 = (f32[768]{0:T(1024)S(1)}, f32[768]{0:T(1024)}, u32[]{:S(2)}) copy-start(f32[768]{0:T(1024)} %param.15) | copy-start | bytes 9220
  830.8 126.3 %copy-start.22 = (f32[768]{0:T(1024)S(1)}, f32[768]{0:T(1024)}, u32[]{:S(2)}) copy-start(f32[768]{0:T(1024)} %param.26) | copy-start | bytes 9220
  (7 other events, 24.4 us)
where the time goes:
time: 1520 us; the launch traced here: 1510 us
  blocking collectives  510 us (34%)
  waiting for transfers between devices  378 us (25%)
  matrix products  367 us (24%)
  local copies, waits for them, and re-layouts  136 us (9%)
  starting transfers between devices  92.8 us (6%)
  other arithmetic  21.4 us (1%)
    psum x1, blocking collectives, ensemble_step(): summed = lax.psum(state_values, 'member')  510 us
    dot_general x1, matrix products, on_device(): jnp.dot(normed2, fc1_weight, preferred_element_type=jnp.float32) + fc1_bias  126 us
    dot_general x12, matrix products, contract(): return jnp.einsum(form, left, right, precision=FULL_PRECISION)  120 us
    all_to_all x1, waiting for transfers between devices, on_device(): lax.all_to_all(imag_part, 'spatial', split_axis=1, concat_axis=0, tiled=T...  95.7 us
    all_to_all x1, waiting for transfers between devices, on_device(): lax.all_to_all(imag_part, 'spatial', split_axis=0, concat_axis=1, tiled=T...  95.6 us
    all_to_all x1, waiting for transfers between devices, on_device(): lax.all_to_all(real_part, 'spatial', split_axis=1, concat_axis=0, tiled=T...  94.8 us
    dot_general x8, matrix products, block_product(): jnp.einsum('...bi,bio->...bo', values, weight, precision=FULL_PRECISION)  92.8 us
    all_to_all x1, waiting for transfers between devices, on_device(): lax.all_to_all(real_part, 'spatial', split_axis=0, concat_axis=1, tiled=T...  91.6 us
  transfers between devices with their start and end apart: 4, of which 4 were waited for; matrix products, arithmetic and copies ran while one was open for 5% of the time, Pallas kernels for 0%

commit v1 on v0

--- a/solution.py
+++ b/solution.py
@@ -1,3 +1,4 @@
+import functools
 import math
 import jax
 import jax.numpy as jnp
@@ -8,6 +9,28 @@
 EPSILON = 1e-06
 SHRINK = 0.01
 FULL_PRECISION = lax.Precision.HIGHEST
+
+
+def store_the_loops(mine, mesh_ax):
+    kept_arr, block_last = (lax.axis_size(mesh_ax), lax.axis_index(mesh_ax))
+    outer = mine.shape[0] // kept_arr
+    k_now = jnp.roll(mine, -block_last * outer, 0)
+    row_list = [lax.slice_in_dim(k_now, 0, outer, axis=0)]
+    for ii in range(1, kept_arr):
+        all_values = lax.slice_in_dim(k_now, ii * outer, (ii + 1) * outer, axis=0)
+        row_list.append(
+            lax.ppermute(
+                all_values,
+                axis_name=mesh_ax,
+                perm=[(d, (d + ii) % kept_arr) for d in range(kept_arr)],
+            )
+        )
+    back = jnp.concatenate(row_list[::-1], axis=1)
+    block_out = jnp.roll(back, (block_last + 1) * row_list[0].shape[1], 1)
+    return block_out
+
+
+expand_pipes = functools.partial(store_the_loops, mesh_ax="spatial")
 
 
 def from_behind(block, axis, distance):
@@ -145,7 +168,7 @@
         real_part, imag_part, spectral_w1, spectral_b1, spectral_w2, spectral_b2
     )
     real_part, imag_part = (
-        lax.all_to_all(real_part, "spatial", split_axis=0, concat_axis=1, tiled=True),
+        expand_pipes(real_part),
         lax.all_to_all(imag_part, "spatial", split_axis=0, concat_axis=1, tiled=True),
     )
     filtered = longitude_inverse(real_part, imag_part, lon_len)

time: 1520 us -> 1560 us (1.026)
  starting transfers between devices: 92.8 us -> 196 us
  waiting for transfers between devices: 378 us -> 305 us
  blocking collectives: 510 us -> 484 us
  local copies, waits for them, and re-layouts: 136 us -> 160 us
    ppermute x0 -> x15, starting transfers between devices: none -> 132 us  [store_the_loops(): lax.ppermute(all_values, axis_name=mesh_ax, perm=[(d, (d + ii) % kept_arr...]
    ppermute x0 -> x15, waiting for transfers between devices: none -> 114 us  [store_the_loops(): lax.ppermute(all_values, axis_name=mesh_ax, perm=[(d, (d + ii) % kept_arr...]
    all_to_all x1, waiting for transfers between devices: 95.6 us -> 0.01 us  [on_device(): lax.all_to_all(imag_part, 'spatial', split_axis=0, concat_axis=1, tiled=T...]
    all_to_all x1 -> x0, waiting for transfers between devices: 91.6 us -> none  [on_device(): lax.all_to_all(real_part, 'spatial', split_axis=0, concat_axis=1, tiled=T...]
    concatenate x0 -> x1, local copies, waits for them, and re-layouts: none -> 37.9 us  [store_the_loops(): block_out = jnp.roll(back, (block_last + 1) * row_list[0].shape[1], 1)]
    all_to_all x1 -> x0, starting transfers between devices: 28.2 us -> none  [on_device(): lax.all_to_all(real_part, 'spatial', split_axis=0, concat_axis=1, tiled=T...]
    psum x1, blocking collectives: 510 us -> 484 us  [ensemble_step(): summed = lax.psum(state_values, 'member')]
    all_to_all x3 -> x0, local copies, waits for them, and re-layouts: 18.4 us -> none  [on_device(): lax.all_to_all(real_part, 'spatial', split_axis=0, concat_axis=1, tiled=T...]
  transfers between devices with their start and end apart: 4 -> 18, of which waited for: 4 -> 8; matrix products, arithmetic and copies ran while one was open for 5% -> 7% of each run, Pallas kernels for 0% -> 0%
where the time goes in v1:
time: 1560 us; the launch traced here: 1550 us
  blocking collectives  484 us (31%)
  matrix products  366 us (23%)
  waiting for transfers between devices  305 us (20%)
  starting transfers between devices  196 us (13%)
  local copies, waits for them, and re-layouts  160 us (10%)
  other arithmetic  36 us (2%)
    psum x1, blocking collectives, ensemble_step(): summed = lax.psum(state_values, 'member')  484 us
    ppermute x15, starting transfers between devices, store_the_loops(): lax.ppermute(all_values, axis_name=mesh_ax, perm=[(d, (d + ii) % kept_arr...  132 us
    dot_general x1, matrix products, on_device(): jnp.dot(normed2, fc1_weight, preferred_element_type=jnp.float32) + fc1_bias  127 us
    dot_general x12, matrix products, contract(): return jnp.einsum(form, left, right, precision=FULL_PRECISION)  121 us
    ppermute x15, waiting for transfers between devices, store_the_loops(): lax.ppermute(all_values, axis_name=mesh_ax, perm=[(d, (d + ii) % kept_arr...  114 us
    all_to_all x1, waiting for transfers between devices, on_device(): lax.all_to_all(imag_part, 'spatial', split_axis=1, concat_axis=0, tiled=T...  95.7 us
    all_to_all x1, waiting for transfers between devices, on_device(): lax.all_to_all(real_part, 'spatial', split_axis=1, concat_axis=0, tiled=T...  94.7 us
    dot_general x8, matrix products, block_product(): jnp.einsum('...bi,bio->...bo', values, weight, precision=FULL_PRECISION)  92.9 us
  transfers between devices with their start and end apart: 18, of which 8 were waited for; matrix products, arithmetic and copies ran while one was open for 7% of the time, Pallas kernels for 0%

profile of v1, /device:TPU:0, one launch (start us, length us, event | category | flops | bytes accessed | tf_op | source)
XLA Modules:
  0.0 1548.4 jit_solution(3744095920029236945)
XLA Ops:
  7.6 9.6 negate_bitcast_fusion
  31.3 12.0 fusion.99
  49.6 95.7 %all-to-all-done.1 = f32[32,64,768]{2,0,1:T(8,128)} async-done(((f32[32,64,768]{2,0,1:T(8,128)}), f32[32,64,768]{2,0,1:T(8,128)}, u32[]{:S(2)}, u32[]{:S(2)}) %all-to-all-start.1) | async-done | bytes 6291488 | tf_op jit(solution)/shard_map/all_to_all | solution.py:165
  145.3 28.5 %all-to-all-start = ((f32[32,64,768]{2,0,1:T(8,128)}), f32[32,64,768]{2,0,1:T(8,128)}, u32[]{:S(2)}, u32[]{:S(2)}) async-start(f32[32,64,768]{2,0,1:T(8,128)} %copy.57), calls=%async_computation | async-start | bytes 12582912 | tf_op jit(solution)/shard_map/all_to_all | solution.py:164
  193.2 94.7 %all-to-all-done = f32[32,64,768]{2,0,1:T(8,128)} async-done(((f32[32,64,768]{2,0,1:T(8,128)}), f32[32,64,768]{2,0,1:T(8,128)}, u32[]{:S(2)}, u32[]{:S(2)}) %all-to-all-start) | async-done | bytes 6291488 | tf_op jit(solution)/shard_map/all_to_all | solution.py:164
  302.2 10.0 reshape.102
  312.2 13.7 fusion.58
  325.9 9.9 fusion.60
  344.0 9.9 reshape.101
  353.9 13.1 add_maximum_fusion
  376.5 9.8 fusion.52
  395.9 14.9 select_bitcast_fusion
  410.9 11.0 copy.70
  421.8 9.6 reshape.104
  431.5 12.4 select_bitcast_fusion.1
  443.9 11.0 copy.69
  486.9 28.1 %all-to-all-start.2 = ((f32[512,4,768]{2,1,0:T(4,128)}), f32[512,4,768]{2,1,0:T(4,128)}, u32[]{:S(2)}, u32[]{:S(2)}) async-start(f32[512,4,768]{2,1,0:T(4,128)} %copy.75), calls=%async_computation.2 | async-start | bytes 12582912 | tf_op jit(solution)/shard_map/all_to_all | solution.py:172
  537.7 9.9 fusion.66
  555.8 74.2 %collective-permute-done.14 = f32[32,4,768]{2,1,0:T(4,128)S(1)} collective-permute-done((f32[32,4,768]{2,1,0:T(4,128)S(1)}, f32[32,4,768]{2,1,0:T(4,128)S(1)}, u32[]{:S(2)}, u32[]{:S(2)}) %collective-permute-start.14) | collective-permute-done | bytes 393248 | tf_op jit(solution)/shard_map/ppermute | solution.py:22
  631.2 63.5 %collective-permute-start.8 = (f32[32,4,768]{2,1,0:T(4,128)S(1)}, f32[32,4,768]{2,1,0:T(4,128)S(1)}, u32[]{:S(2)}, u32[]{:S(2)}) collective-permute-start(f32[32,4,768]{2,1,0:T(4,128)S(1)} %get-tuple-element.10), channel_id=1, source_target_pairs={{0,7},{1,8},{2,9},{3,10},{4,11},{5,12},{6,13},{7,14},{8,15},{9,0},... | collective-permute-start | bytes 1179656 | tf_op jit(solution)/shard_map/ppermute | solution.py:22
  697.5 28.4 %collective-permute-done.10 = f32[32,4,768]{2,1,0:T(4,128)S(1)} collective-permute-done((f32[32,4,768]{2,1,0:T(4,128)S(1)}, f32[32,4,768]{2,1,0:T(4,128)S(1)}, u32[]{:S(2)}, u32[]{:S(2)}) %collective-permute-start.10) | collective-permute-done | bytes 393248 | tf_op jit(solution)/shard_map/ppermute | solution.py:22
  727.1 10.7 collective-permute-start.4
  737.9 22.4 %collective-permute-start.3 = (f32[32,4,768]{2,1,0:T(4,128)}, f32[32,4,768]{2,1,0:T(4,128)}, u32[]{:S(2)}, u32[]{:S(2)}) collective-permute-start(f32[32,4,768]{2,1,0:T(4,128)} %get-tuple-element.15), channel_id=1, source_target_pairs={{0,12},{1,13},{2,14},{3,15},{4,0},{5,1},{6,2},{7,3},{8,4},{9,5},{1... | collective-permute-start | bytes 1179656 | tf_op jit(solution)/shard_map/ppermute | solution.py:22
  761.6 13.3 collective-permute-start.1
  774.9 11.8 collective-permute-start
  795.9 37.9 %concatenate.11 = f32[32,128,768]{2,1,0:T(8,128)} concatenate(f32[32,4,768]{2,1,0:T(4,128)} %collective-permute-done, f32[32,4,768]{2,1,0:T(4,128)} %collective-permute-done.1, f32[32,4,768]{2,1,0:T(4,128)} %collective-permute-done.2, f32[32,4,768]{2,1,0:T(4,128)} %collective-permute-done.3, f32[32,4,768]{2,1,0:T(4,128)} %collective-permute-done.4, ...), dimensions={1} | concatenate | bytes 25165824 | tf_op jit(solution)/shard_map/jit(_roll_dynamic)/concatenate | solution.py:29
  852.4 15.5 %fusion.126 = f32[128,32,768]{2,0,1:T(8,128)} fusion(f32[32,64,768]{2,1,0:T(8,128)} %all_to_all.44, f32[64]{0:T(128)S(1)} %fusion.189), kind=kOutput, calls=%fused_computation.141 | convolution fusion | flops 2416041984 | bytes 18874624 | tf_op jit(solution)/shard_map/rkd,lk->rld/dot_general | solution.py:55
  868.0 21.3 %fusion.268 = (f32[32,128]{1,0:T(8,128)S(1)}, f32[32,128,768]{2,1,0:T(8,128)}) fusion(f32[768]{0:T(1024)S(1)} %copy-done.18, f32[768]{0:T(1024)S(1)} %copy-done.20, f32[32,128]{1,0:T(8,128)S(1)} %copy-done.14, f32[32,128]{1,0:T(8,128)S(1)} %copy-done.12, bf16[32,128,768]{2,1,0:T(8,128)(2,1)S(1)} %bitcast.181, f32[128,32,768]{2,0,1:T(8,128)} %fusion.126, ...), kind=kOutput, calls=%fused_computation.282 | convolution fusion | flops 2444349440 | bytes 37804292 | tf_op jit(solution)/shard_map/rkd,lk->rld/dot_general | solution.py:55
  899.9 126.6 %fusion.2.clone.6 = bf16[4096,3072]{1,0:T(8,128)(2,1)} fusion(bf16[4096,768]{1,0:T(8,128)(2,1)S(1)} %fusion.47, bf16[768,3072]{1,0:T(8,128)(2,1)} %param.23, f32[3072]{0:T(1024)S(1)} %copy-done.23), kind=kOutput, calls=%fused_computation.3.clone.clone.clone.clone.clone.1 | convolution fusion | flops 20157825024 | bytes 36188160 | tf_op jit(solution)/shard_map/dot_general | solution.py:178
  1026.5 25.9 %fusion.49 = bf16[4096,768]{1,0:T(8,128)(2,1)} fusion(f32[32,128,768]{2,1,0:T(8,128)S(1)} %copy-done.1, bf16[3072,768]{1,0:T(8,128)(2,1)} %param.25, f32[768]{0:T(1024)S(1)} %copy-done.24, bf16[4096,3072]{1,0:T(8,128)(2,1)} %fusion.2.clone.6), kind=kOutput, calls=%fused_computation.63 | convolution fusion | flops 19336790016 | bytes 48761856 | tf_op jit(solution)/shard_map/dot_general | solution.py:181
  1052.5 484.2 %all-reduce.1 = f32[32,128,768]{2,1,0:T(8,128)} all-reduce(bf16[32,128,768]{2,1,0:T(8,128)(2,1)} %bitcast.199), channel_id=1, replica_groups=mesh['groups'=2,'member'=8,'half'=2] {'member'}, use_global_device_ids=true, to_apply=%region_4.6 | all-reduce | flops 3145728 | bytes 18874368 | tf_op jit(solution)/shard_map/psum | solution.py:188
  1536.7 11.2 subtract_convert_fusion
  (144 shorter events, 195.8 us)
Async XLA Ops:
  5.2 26.0 %copy-start.11 = (f32[32,128]{1,0:T(8,128)}, f32[32,128]{1,0:T(8,128)S(1)}, u32[]{:S(2)}) copy-start(f32[32,128]{1,0:T(8,128)S(1)} %broadcast_multiply_fusion.1) | copy-start | bytes 49156
  7.6 23.6 %copy-start.13 = (f32[32,128]{1,0:T(8,128)}, f32[32,128]{1,0:T(8,128)S(1)}, u32[]{:S(2)}) copy-start(f32[32,128]{1,0:T(8,128)S(1)} %add_rsqrt_fusion) | copy-start | bytes 49156
  23.8 121.5 %all-to-all-start.1 = ((f32[32,64,768]{2,0,1:T(8,128)}), f32[32,64,768]{2,0,1:T(8,128)}, u32[]{:S(2)}, u32[]{:S(2)}) async-start(f32[32,64,768]{2,0,1:T(8,128)} %copy.60), calls=%async_computation.1 | async-start | bytes 12582912 | tf_op jit(solution)/shard_map/all_to_all | solution.py:165
  49.6 124.2 %copy-start.15 = (f32[2,8,96]{2,1,0:T(8,128)S(1)}, f32[2,8,96]{2,1,0:T(8,128)}, u32[]{:S(2)}) copy-start(f32[2,8,96]{2,1,0:T(8,128)} %param.18) | copy-start | bytes 18436
  49.6 124.3 %copy-start.16 = (f32[2,8,96]{2,1,0:T(8,128)S(1)}, f32[2,8,96]{2,1,0:T(8,128)}, u32[]{:S(2)}) copy-start(f32[2,8,96]{2,1,0:T(8,128)} %param.20) | copy-start | bytes 18436
  145.3 142.6 %all-to-all-start = ((f32[32,64,768]{2,0,1:T(8,128)}), f32[32,64,768]{2,0,1:T(8,128)}, u32[]{:S(2)}, u32[]{:S(2)}) async-start(f32[32,64,768]{2,0,1:T(8,128)} %copy.57), calls=%async_computation | async-start | bytes 12582912 | tf_op jit(solution)/shard_map/all_to_all | solution.py:164
  193.2 101.1 %slice-start.12 = ((s8[6291456]{0:T(1024)(128)(4,1)}), s8[2097152]{0:T(1024)(128)(4,1)S(1)}, s32[]{:S(2)}) async-start(s8[6291456]{0:T(1024)(128)(4,1)} %bitcast.197), calls=%async_computation.15 | async-start | bytes 4194304
  312.2 23.6 %slice-start.6 = ((s8[6291456]{0:T(1024)(128)(4,1)}), s8[4194304]{0:T(1024)(128)(4,1)S(1)}, s32[]{:S(2)}) async-start(s8[6291456]{0:T(1024)(128)(4,1)} %bitcast.187), calls=%async_computation.9 | async-start | bytes 8388608
  312.2 23.6 %slice-start.10 = ((s8[6291456]{0:T(1024)(128)(4,1)}), s8[4194304]{0:T(1024)(128)(4,1)S(1)}, s32[]{:S(2)}) async-start(s8[6291456]{0:T(1024)(128)(4,1)} %bitcast.195), calls=%async_computation.13 | async-start | bytes 8388608
  367.0 19.2 %slice-start = ((s8[8388608]{0:T(1024)(128)(4,1)}), s8[4194304]{0:T(1024)(128)(4,1)S(1)}, s32[]{:S(2)}) async-start(s8[8388608]{0:T(1024)(128)(4,1)} %bitcast.178), calls=%async_computation.3 | async-start | bytes 8388608
  367.1 19.2 %slice-start.8 = ((s8[8388608]{0:T(1024)(128)(4,1)}), s8[4194304]{0:T(1024)(128)(4,1)S(1)}, s32[]{:S(2)}) async-start(s8[8388608]{0:T(1024)(128)(4,1)} %bitcast.190), calls=%async_computation.11 | async-start | bytes 8388608
  486.9 346.9 %all-to-all-start.2 = ((f32[512,4,768]{2,1,0:T(4,128)}), f32[512,4,768]{2,1,0:T(4,128)}, u32[]{:S(2)}, u32[]{:S(2)}) async-start(f32[512,4,768]{2,1,0:T(4,128)} %copy.75), calls=%async_computation.2 | async-start | bytes 12582912 | tf_op jit(solution)/shard_map/all_to_all | solution.py:172
  550.0 80.1 %collective-permute-start.14 = (f32[32,4,768]{2,1,0:T(4,128)S(1)}, f32[32,4,768]{2,1,0:T(4,128)S(1)}, u32[]{:S(2)}, u32[]{:S(2)}) collective-permute-start(f32[32,4,768]{2,1,0:T(4,128)S(1)} %get-tuple-element.4), channel_id=1, source_target_pairs={{0,1},{1,2},{2,3},{3,4},{4,5},{5,6},{6,7},{7,8},{8,9},{9,10},{10,1... | collective-permute-start | bytes 1179656 | tf_op jit(solution)/shard_map/ppermute | solution.py:22
  550.3 81.0 %collective-permute-start.13 = (f32[32,4,768]{2,1,0:T(4,128)S(1)}, f32[32,4,768]{2,1,0:T(4,128)S(1)}, u32[]{:S(2)}, u32[]{:S(2)}) collective-permute-start(f32[32,4,768]{2,1,0:T(4,128)S(1)} %get-tuple-element.5), channel_id=1, source_target_pairs={{0,2},{1,3},{2,4},{3,5},{4,6},{5,7},{6,8},{7,9},{8,10},{9,11},{10,... | collective-permute-start | bytes 1179656 | tf_op jit(solution)/shard_map/ppermute | solution.py:22
  552.0 142.7 %collective-permute-start.12 = (f32[32,4,768]{2,1,0:T(4,128)S(1)}, f32[32,4,768]{2,1,0:T(4,128)S(1)}, u32[]{:S(2)}, u32[]{:S(2)}) collective-permute-start(f32[32,4,768]{2,1,0:T(4,128)S(1)} %get-tuple-element.6), channel_id=1, source_target_pairs={{0,3},{1,4},{2,5},{3,6},{4,7},{5,8},{6,9},{7,10},{8,11},{9,12},{10... | collective-permute-start | bytes 1179656 | tf_op jit(solution)/shard_map/ppermute | solution.py:22
  554.3 140.4 %collective-permute-start.11 = (f32[32,4,768]{2,1,0:T(4,128)S(1)}, f32[32,4,768]{2,1,0:T(4,128)S(1)}, u32[]{:S(2)}, u32[]{:S(2)}) collective-permute-start(f32[32,4,768]{2,1,0:T(4,128)S(1)} %get-tuple-element.7), channel_id=1, source_target_pairs={{0,4},{1,5},{2,6},{3,7},{4,8},{5,9},{6,10},{7,11},{8,12},{9,13},{1... | collective-permute-start | bytes 1179656 | tf_op jit(solution)/shard_map/ppermute | solution.py:22
  555.7 170.2 %collective-permute-start.10 = (f32[32,4,768]{2,1,0:T(4,128)S(1)}, f32[32,4,768]{2,1,0:T(4,128)S(1)}, u32[]{:S(2)}, u32[]{:S(2)}) collective-permute-start(f32[32,4,768]{2,1,0:T(4,128)S(1)} %get-tuple-element.8), channel_id=1, source_target_pairs={{0,5},{1,6},{2,7},{3,8},{4,9},{5,10},{6,11},{7,12},{8,13},{9,14},{... | collective-permute-start | bytes 1179656 | tf_op jit(solution)/shard_map/ppermute | solution.py:22
  630.1 97.1 %collective-permute-start.9 = (f32[32,4,768]{2,1,0:T(4,128)S(1)}, f32[32,4,768]{2,1,0:T(4,128)S(1)}, u32[]{:S(2)}, u32[]{:S(2)}) collective-permute-start(f32[32,4,768]{2,1,0:T(4,128)S(1)} %get-tuple-element.9), channel_id=1, source_target_pairs={{0,6},{1,7},{2,8},{3,9},{4,10},{5,11},{6,12},{7,13},{8,14},{9,15},... | collective-permute-start | bytes 1179656 | tf_op jit(solution)/shard_map/ppermute | solution.py:22
  631.2 106.7 %collective-permute-start.8 = (f32[32,4,768]{2,1,0:T(4,128)S(1)}, f32[32,4,768]{2,1,0:T(4,128)S(1)}, u32[]{:S(2)}, u32[]{:S(2)}) collective-permute-start(f32[32,4,768]{2,1,0:T(4,128)S(1)} %get-tuple-element.10), channel_id=1, source_target_pairs={{0,7},{1,8},{2,9},{3,10},{4,11},{5,12},{6,13},{7,14},{8,15},{9,0},... | collective-permute-start | bytes 1179656 | tf_op jit(solution)/shard_map/ppermute | solution.py:22
  694.7 65.6 %collective-permute-start.7 = (f32[32,4,768]{2,1,0:T(4,128)S(1)}, f32[32,4,768]{2,1,0:T(4,128)}, u32[]{:S(2)}, u32[]{:S(2)}) collective-permute-start(f32[32,4,768]{2,1,0:T(4,128)S(1)} %get-tuple-element.11), channel_id=1, source_target_pairs={{0,8},{1,9},{2,10},{3,11},{4,12},{5,13},{6,14},{7,15},{8,0},{9,1},... | collective-permute-start | bytes 1179656 | tf_op jit(solution)/shard_map/ppermute | solution.py:22
  694.7 66.9 %collective-permute-start.6 = (f32[32,4,768]{2,1,0:T(4,128)S(1)}, f32[32,4,768]{2,1,0:T(4,128)}, u32[]{:S(2)}, u32[]{:S(2)}) collective-permute-start(f32[32,4,768]{2,1,0:T(4,128)S(1)} %get-tuple-element.12), channel_id=1, source_target_pairs={{0,9},{1,10},{2,11},{3,12},{4,13},{5,14},{6,15},{7,0},{8,1},{9,2},... | collective-permute-start | bytes 1179656 | tf_op jit(solution)/shard_map/ppermute | solution.py:22
  725.9 49.0 %collective-permute-start.5 = (f32[32,4,768]{2,1,0:T(4,128)S(1)}, f32[32,4,768]{2,1,0:T(4,128)}, u32[]{:S(2)}, u32[]{:S(2)}) collective-permute-start(f32[32,4,768]{2,1,0:T(4,128)S(1)} %get-tuple-element.13), channel_id=1, source_target_pairs={{0,10},{1,11},{2,12},{3,13},{4,14},{5,15},{6,0},{7,1},{8,2},{9,3},... | collective-permute-start | bytes 1179656 | tf_op jit(solution)/shard_map/ppermute | solution.py:22
  727.1 59.6 %collective-permute-start.4 = (f32[32,4,768]{2,1,0:T(4,128)}, f32[32,4,768]{2,1,0:T(4,128)}, u32[]{:S(2)}, u32[]{:S(2)}) collective-permute-start(f32[32,4,768]{2,1,0:T(4,128)} %get-tuple-element.14), channel_id=1, source_target_pairs={{0,11},{1,12},{2,13},{3,14},{4,15},{5,0},{6,1},{7,2},{8,3},{9,4},{... | collective-permute-start | bytes 1179656 | tf_op jit(solution)/shard_map/ppermute | solution.py:22
  737.9 48.8 %collective-permute-start.3 = (f32[32,4,768]{2,1,0:T(4,128)}, f32[32,4,768]{2,1,0:T(4,128)}, u32[]{:S(2)}, u32[]{:S(2)}) collective-permute-start(f32[32,4,768]{2,1,0:T(4,128)} %get-tuple-element.15), channel_id=1, source_target_pairs={{0,12},{1,13},{2,14},{3,15},{4,0},{5,1},{6,2},{7,3},{8,4},{9,5},{1... | collective-permute-start | bytes 1179656 | tf_op jit(solution)/shard_map/ppermute | solution.py:22
  760.3 26.4 %collective-permute-start.2 = (f32[32,4,768]{2,1,0:T(4,128)}, f32[32,4,768]{2,1,0:T(4,128)}, u32[]{:S(2)}, u32[]{:S(2)}) collective-permute-start(f32[32,4,768]{2,1,0:T(4,128)} %get-tuple-element.16), channel_id=1, source_target_pairs={{0,13},{1,14},{2,15},{3,0},{4,1},{5,2},{6,3},{7,4},{8,5},{9,6},{10... | collective-permute-start | bytes 1179656 | tf_op jit(solution)/shard_map/ppermute | solution.py:22
  761.6 31.2 %collective-permute-start.1 = (f32[32,4,768]{2,1,0:T(4,128)}, f32[32,4,768]{2,1,0:T(4,128)}, u32[]{:S(2)}, u32[]{:S(2)}) collective-permute-start(f32[32,4,768]{2,1,0:T(4,128)} %get-tuple-element.17), channel_id=1, source_target_pairs={{0,14},{1,15},{2,0},{3,1},{4,2},{5,3},{6,4},{7,5},{8,6},{9,7},{10,... | collective-permute-start | bytes 1179656 | tf_op jit(solution)/shard_map/ppermute | solution.py:22
  774.9 21.0 %collective-permute-start = (f32[32,4,768]{2,1,0:T(4,128)}, f32[32,4,768]{2,1,0:T(4,128)}, u32[]{:S(2)}, u32[]{:S(2)}) collective-permute-start(f32[32,4,768]{2,1,0:T(4,128)} %get-tuple-element.18), channel_id=1, source_target_pairs={{0,15},{1,0},{2,1},{3,2},{4,3},{5,4},{6,5},{7,6},{8,7},{9,8},{10,9... | collective-permute-start | bytes 1179656 | tf_op jit(solution)/shard_map/ppermute | solution.py:22
  844.6 23.4 %slice-start.2 = ((s8[6291456]{0:T(1024)(128)(4,1)}), s8[2097152]{0:T(1024)(128)(4,1)S(1)}, s32[]{:S(2)}) async-start(s8[6291456]{0:T(1024)(128)(4,1)} %bitcast.180), calls=%async_computation.5 | async-start | bytes 4194304
  852.4 15.5 %copy-start.18 = (f32[768]{0:T(1024)S(1)}, f32[768]{0:T(1024)}, u32[]{:S(2)}) copy-start(f32[768]{0:T(1024)} %param.16) | copy-start | bytes 9220
  852.4 15.5 %copy-start.20 = (f32[768]{0:T(1024)S(1)}, f32[768]{0:T(1024)}, u32[]{:S(2)}) copy-start(f32[768]{0:T(1024)} %param.15) | copy-start | bytes 9220
  899.9 126.6 %copy-start.1 = (f32[32,128,768]{2,1,0:T(8,128)S(1)}, f32[32,128,768]{2,1,0:T(8,128)}, u32[]{:S(2)}) copy-start(f32[32,128,768]{2,1,0:T(8,128)} %get-tuple-element.26) | copy-start | bytes 37748740
  899.9 126.6 %copy-start.24 = (f32[768]{0:T(1024)S(1)}, f32[768]{0:T(1024)}, u32[]{:S(2)}) copy-start(f32[768]{0:T(1024)} %param.26) | copy-start | bytes 9220
  (25 other events, 237.6 us)
